TPU v7x, 256 devices: a whole 4x4x8 slice. The times are simulated.
256 devices in a mesh: mp: 4 (over z_lo, core), fsdp: 16 (over y, x), dp: 4 (over z_hi).
Axes of the slice: x: 4, y: 4, z: 8 (z_hi: 4, z_lo: 2; z = z_hi * 2 + z_lo), core: 2. Of those that a mesh axis runs over, the one named last changes fastest.
Arguments:
- gen_noise: float32 [4, 4096, 128], P('dp', 'fsdp'), may hold values from -6 to 6
- renoise: float32 [4, 4096, 128], P('dp', 'fsdp'), may hold values from -120 to 120
- gen_step: int32 [4], P('dp'), may hold values from 250 to 999
- renoise_step: int32 [4], P('dp'), may hold values from 20 to 979
- text_pooled: bfloat16 [4, 768], P('dp'), may hold values from -6 to 6
- embed: bfloat16 [3, 64, 3072], replicated, may hold values from -0.75 to 0.75
- mod_weight: bfloat16 [3, 1024, 6144], P(None, None, 'fsdp'), may hold values from -0.1875 to 0.1875
- proj_weight: bfloat16 [3, 3072, 3072], P(None, 'fsdp', 'mp'), may hold values from -0.109375 to 0.109375
- unembed: bfloat16 [3, 64, 3072], P(None, None, 'mp'), may hold values from -0.109375 to 0.109375
Outputs:
- gen_grad: float32 [3072, 3072], P('fsdp', 'mp')
- score_gap: float32 [4, 4096, 128], P('dp', 'fsdp')
All inputs are finite; a program needn't handle non-finite values. Where the computation divides by a largest or mean magnitude, that divisor is 1e-20 or more.
Results may differ from a plain program's by a relative error of at most 0.03.
Values may be sent and summed in bfloat16 or wider, within the bound.
A program may use at most 128 MiB of HBM per device.

v0:
```python
import math

import jax
import jax.numpy as jnp
from jax import lax
from jax.sharding import PartitionSpec as P

D = 3072
CH = 64
TEMB = 256


GUIDANCE = 3.5
EPS_NORM = 1e-06
EPS_GAP = 1e-05


def sinusoid(timesteps):
    half_size = TEMB // 2
    frequency = jnp.exp(-math.log(10000.0) * jnp.arange(half_size, dtype=jnp.float32) / half_size)
    angles = timesteps.astype(jnp.float32)[:, None] * frequency[None, :]
    return jnp.concatenate([jnp.cos(angles), jnp.sin(angles)], axis=1)


def condition(timesteps, pooled):
    joined = jnp.concatenate([sinusoid(timesteps), pooled.astype(jnp.float32)], axis=1)
    return jax.nn.silu(joined).astype(jnp.bfloat16)


def normalize(values):
    average = jnp.mean(values, axis=1, keepdims=True)
    centred = values - average
    variance = jnp.mean(centred * centred, axis=1, keepdims=True)
    return centred * lax.rsqrt(variance + EPS_NORM)


def modulate(normed, modulation):
    return (normed * (1.0 + modulation[D:]) + modulation[:D]).astype(jnp.bfloat16)


def unembed_part(residual_sum, out_weight):
    return lax.dot_general(
        residual_sum.astype(jnp.bfloat16),
        out_weight,
        (((1,), (1,)), ((), ())),
        preferred_element_type=jnp.float32,
    )


def row_product(hidden, weight_piece):
    return jnp.dot(hidden, weight_piece, preferred_element_type=jnp.float32)


def body(
    gen_noise, renoise, gen_step, renoise_step, text_pooled, embed, mod_weight, proj_weight, unembed
):
    quarter = proj_weight.shape[2]
    col_start = lax.axis_index("mp") * quarter
    blank_text = jnp.zeros_like(text_pooled)
    noisy_vec = condition(renoise_step, text_pooled)
    local_mod = jnp.concatenate(
        [
            jnp.dot(
                condition(gen_step, text_pooled), mod_weight[0], preferred_element_type=jnp.float32
            ),
            jnp.dot(noisy_vec, mod_weight[1], preferred_element_type=jnp.float32),
            jnp.dot(
                condition(renoise_step, blank_text),
                mod_weight[1],
                preferred_element_type=jnp.float32,
            ),
            jnp.dot(noisy_vec, mod_weight[2], preferred_element_type=jnp.float32),
        ],
        axis=0,
    )
    modulation = lax.all_gather(local_mod, "fsdp", axis=1, tiled=True)
    latent = gen_noise[0].reshape(-1, CH)
    latent_bf = latent.astype(jnp.bfloat16)
    token_rows = latent.shape[0]
    embedded = jnp.dot(latent_bf, embed[0], preferred_element_type=jnp.float32)
    gen_hidden = modulate(normalize(embedded), modulation[0])
    gen_part = row_product(gen_hidden, lax.all_gather(proj_weight[0], "fsdp", axis=0, tiled=True))
    gen_cols = lax.dynamic_slice_in_dim(embedded, col_start, quarter, 1)
    clean_part = unembed_part(gen_cols + gen_part, unembed[0]).reshape(-1, 2 * CH)
    clean_lat = lax.psum(clean_part, "mp")
    noise_level = renoise_step[0].astype(jnp.float32) / 1000.0
    noisy_lat = (1.0 - noise_level) * clean_lat + noise_level * renoise[0]
    noisy_bf = noisy_lat.reshape(-1, CH).astype(jnp.bfloat16)
    teacher_in = jnp.dot(noisy_bf, embed[1], preferred_element_type=jnp.float32)
    teacher_norm = normalize(teacher_in)
    cond_hidden = modulate(teacher_norm, modulation[1])
    blank_hidden = modulate(teacher_norm, modulation[2])
    fake_in = jnp.dot(noisy_bf, embed[2], preferred_element_type=jnp.float32)
    fake_hidden = modulate(normalize(fake_in), modulation[3])
    pieces = (
        lax.all_gather(proj_weight[1], "fsdp", axis=0, tiled=True),
        lax.all_gather(proj_weight[2], "fsdp", axis=0, tiled=True),
    )
    cond_part = row_product(cond_hidden, pieces[0])
    blank_part = row_product(blank_hidden, pieces[0])
    fake_part = row_product(fake_hidden, pieces[1])
    teacher_cols = lax.dynamic_slice_in_dim(teacher_in, col_start, quarter, 1)
    fake_cols = lax.dynamic_slice_in_dim(fake_in, col_start, quarter, 1)
    cond_out, blank_out, fake_out = (
        lax.psum(
            unembed_part(teacher_cols + cond_part, unembed[1])
            .reshape(-1, 2 * CH)
            .astype(jnp.bfloat16),
            "mp",
        ).astype(jnp.float32),
        lax.psum(
            unembed_part(teacher_cols + blank_part, unembed[1])
            .reshape(-1, 2 * CH)
            .astype(jnp.bfloat16),
            "mp",
        ).astype(jnp.float32),
        lax.psum(
            unembed_part(fake_cols + fake_part, unembed[2])
            .reshape(-1, 2 * CH)
            .astype(jnp.bfloat16),
            "mp",
        ).astype(jnp.float32),
    )
    real_pred = noisy_lat - noise_level * (blank_out + GUIDANCE * (cond_out - blank_out))
    fake_pred = noisy_lat - noise_level * fake_out
    seq_len = token_rows * lax.axis_size("fsdp")
    gap_total = lax.psum(jnp.sum(jnp.abs(clean_lat - real_pred)), "fsdp")
    gap_scale = gap_total / (seq_len * CH) + EPS_GAP
    score_gap = (fake_pred - real_pred) / gap_scale
    all_tokens = seq_len * lax.axis_size("dp")
    cotangent = (score_gap / math.sqrt(all_tokens)).astype(jnp.bfloat16).reshape(-1, CH)
    upstream = jnp.dot(cotangent, unembed[0], preferred_element_type=jnp.float32).astype(
        jnp.bfloat16
    )
    row_terms = lax.psum_scatter(
        lax.dot_general(
            gen_hidden, upstream, (((0,), (0,)), ((), ())), preferred_element_type=jnp.float32
        ).astype(jnp.bfloat16),
        "fsdp",
        scatter_dimension=0,
        tiled=True,
    )
    gen_grad = lax.psum(row_terms, "dp").astype(jnp.float32)
    return (gen_grad, score_gap[None])


def solution(mesh):
    return jax.shard_map(
        body,
        mesh=mesh,
        in_specs=(
            P("dp", "fsdp", None),
            P("dp", "fsdp", None),
            P("dp"),
            P("dp"),
            P("dp", None),
            P(),
            P(None, None, "fsdp"),
            P(None, "fsdp", "mp"),
            P(None, None, "mp"),
        ),
        out_specs=(P("fsdp", "mp"), P("dp", "fsdp", None)),
        check_vma=False,
    )
```

profile of v0, /device:TPU:1, one launch (start us, length us, event | category | flops | bytes accessed | tf_op | source)
XLA Modules:
  0.0 497.4 jit_solution(18427168380381059458)
XLA Ops:
  7.2 2.1 fusion.104
  9.4 0.9 convert_element_type.109
  10.3 0.1 convert_element_type.110
  11.8 0.7 convert_reduce_fusion
  12.6 1.3 fusion.49
  13.9 1.3 fusion.53
  15.2 1.3 fusion.51
  16.6 1.3 fusion.55
  18.0 20.2 %all_gather.12 = f32[4,6144]{1,0:T(4,128)S(1)} all-gather(f32[4,384]{1,0:T(4,128)S(1)} %pad_maximum_fusion), channel_id=1, replica_groups=mesh['mp'=4,'fsdp'=16,'dp'=4] {'fsdp'}, dimensions={1}, use_global_device_ids=true | all-gather | bytes 104448 | tf_op jit(solution)/shard_map/all_gather | solution.py:76
  38.2 2.1 fusion.105
  40.3 2.6 copy-done
  43.0 0.8 multiply_reduce_fusion.2
  43.7 0.1 slice_add_fusion.1
  43.8 29.5 %all-gather.7.cloned.1.call-done = bf16[1,3072,768]{2,1,0:T(8,128)(2,1)} async-done(((bf16[1,192,768]{2,1,0:T(8,128)(2,1)}), bf16[1,3072,768]{2,1,0:T(8,128)(2,1)}) %all-gather.7.cloned.1.call-update) | async-done | bytes 4718608 | tf_op jit(solution)/shard_map/all_gather | solution.py:82
  73.3 7.9 %fusion.38 = f32[512,64]{1,0:T(8,128)S(1)} fusion(f32[512,3072]{1,0:T(8,128)} %copy-done, s32[]{:T(128)S(6)} %select_n.2, bf16[1,3072,768]{2,1,0:T(8,128)(2,1)} %all-gather.7.cloned.1.call-done, bf16[3,64,768]{2,1,0:T(8,128)(2,1)S(1)} %copy-done.6, f32[3072]{0:T(1024)S(1)} %bitcast.103, f32[3072]{0:T(1024)S(1)} %bitcast.105, f32[512]{0:T(512)S(1)} %add_rsqrt_fusion.2, ...), kind=kOutput, calls=%fused_computation.36 | convolution fusion | flops 2474901504 | bytes 12840964 | tf_op jit(solution)/shard_map/dot_general | solution.py:42
  81.2 0.8 reshape.200
  82.0 0.7 all-gather.9.cloned.1.call-update
  82.7 0.5 all-gather.11.cloned.1.call-update
  83.3 0.2 all-reduce.9.cloned.1.call-start
  83.5 39.2 %all-reduce.5.cloned.1.call-done = f32[256,128]{1,0:T(8,128)} async-done(((f32[256,128]{1,0:T(8,128)}), f32[256,128]{1,0:T(8,128)}) %all-reduce.5.cloned.1.call-update) | async-done | bytes 131088 | tf_op jit(solution)/shard_map/psum | solution.py:85
  122.7 0.9 fusion.85
  123.6 0.1 convert_element_type.120
  123.7 1.0 fusion.106
  124.8 2.7 copy-done.2
  127.5 0.8 multiply_reduce_fusion.1
  128.2 56.2 %all-gather.9.cloned.1.call-done = bf16[1,3072,768]{2,1,0:T(8,128)(2,1)} async-done(((bf16[1,192,768]{2,1,0:T(8,128)(2,1)}), bf16[1,3072,768]{2,1,0:T(8,128)(2,1)}) %all-gather.9.cloned.1.call-update) | async-done | bytes 4718608 | tf_op jit(solution)/shard_map/all_gather | solution.py:97
  184.4 7.9 %fusion.46 = bf16[512,64]{0,1:T(8,128)(2,1)S(1)} fusion(f32[512,3072]{1,0:T(8,128)} %copy-done.2, s32[]{:T(128)S(6)} %select_n.2, bf16[1,3072,768]{2,1,0:T(8,128)(2,1)} %all-gather.9.cloned.1.call-done, f32[3072]{0:T(1024)S(1)} %bitcast.111, f32[3072]{0:T(1024)S(1)} %bitcast.112, f32[512]{0:T(512)S(1)} %add_rsqrt_fusion.1, ...), kind=kOutput, calls=%fused_computation.39 | convolution fusion | flops 2474934272 | bytes 12775428 | tf_op jit(solution)/shard_map/dot_general | solution.py:42
  192.3 0.1 copy.12
  192.5 0.8 convert_element_type.124
  193.2 1.0 fusion.107
  194.3 2.7 copy-done.1
  196.9 0.8 multiply_reduce_fusion
  197.7 48.7 %all-gather.11.cloned.1.call-done = bf16[1,3072,768]{2,1,0:T(8,128)(2,1)} async-done(((bf16[1,192,768]{2,1,0:T(8,128)(2,1)}), bf16[1,3072,768]{2,1,0:T(8,128)(2,1)}) %all-gather.11.cloned.1.call-update) | async-done | bytes 4718608 | tf_op jit(solution)/shard_map/all_gather | solution.py:96
  246.4 7.9 %fusion.40 = bf16[512,64]{0,1:T(8,128)(2,1)S(1)} fusion(f32[512,3072]{1,0:T(8,128)} %copy-done.1, s32[]{:T(128)S(6)} %select_n.2, bf16[1,3072,768]{2,1,0:T(8,128)(2,1)} %all-gather.11.cloned.1.call-done, f32[3072]{0:T(1024)S(1)} %bitcast.109, f32[3072]{0:T(1024)S(1)} %bitcast.110, f32[512]{0:T(512)S(1)} %add_rsqrt_fusion, ...), kind=kOutput, calls=%fused_computation.37 | convolution fusion | flops 2474934272 | bytes 12775428 | tf_op jit(solution)/shard_map/dot_general | solution.py:42
  254.3 0.1 copy.14
  254.4 0.8 convert_element_type.134
  255.2 7.9 %fusion.43 = bf16[512,64]{0,1:T(8,128)(2,1)S(1)} fusion(f32[512,3072]{1,0:T(8,128)} %copy-done.1, s32[]{:T(128)S(6)} %select_n.2, bf16[1,3072,768]{2,1,0:T(8,128)(2,1)} %all-gather.11.cloned.1.call-done, f32[3072]{0:T(1024)S(1)} %bitcast.108, f32[3072]{0:T(1024)S(1)} %bitcast.107, f32[512]{0:T(512)S(1)} %add_rsqrt_fusion, ...), kind=kOutput, calls=%fused_computation.38 | convolution fusion | flops 2474934272 | bytes 12775428 | tf_op jit(solution)/shard_map/dot_general | solution.py:42
  263.1 0.1 copy.13
  263.2 0.8 convert_element_type.129
  264.0 41.0 %all-reduce.9.cloned.1.call-done = (bf16[256,128]{1,0:T(8,128)(2,1)}, bf16[256,128]{1,0:T(8,128)(2,1)}, bf16[256,128]{1,0:T(8,128)(2,1)}) async-done(((bf16[256,128]{1,0:T(8,128)(2,1)}, bf16[256,128]{1,0:T(8,128)(2,1)}, bf16[256,128]{1,0:T(8,128)(2,1)}), (bf16[256,128]{1,0:T(8,128)(2,1)}, bf16[256,128]{1,0:T(8,128)(2,1)}, bf16[256,128]{1,0:T(8,128)(2,1)})) %all-reduce.9.cloned.1.call-update) | async-done | bytes 196624 | tf_op jit(solution)/shard_map/psum | solution.py:117
  305.1 1.5 abs_reduce_fusion
  306.6 34.0 %psum.46 = f32[]{:T(128)} all-reduce(f32[]{:T(128)} %abs_reduce_fusion), channel_id=1, replica_groups=mesh['mp'=4,'fsdp'=16,'dp'=4] {'fsdp'}, use_global_device_ids=true, to_apply=%region_11.12 | all-reduce | flops 1 | bytes 8 | tf_op jit(solution)/shard_map/psum | solution.py:127
  341.2 1.6 multiply_convert_fusion
  342.9 0.1 reshape.201
  343.0 8.2 %convolution_convert_fusion = bf16[3072,768]{1,0:T(8,128)(2,1)} fusion(bf16[512,64]{1,0:T(8,128)(2,1)S(1)} %reshape.201, bf16[3,64,768]{2,1,0:T(8,128)(2,1)S(1)} %copy-done.6, f32[512,3072]{1,0:T(8,128)} %copy-done, f32[3072]{0:T(1024)S(1)} %bitcast.104, f32[3072]{0:T(1024)S(1)} %bitcast.106, f32[512]{0:T(512)S(1)} %add_rsqrt_fusion.2, ...), kind=kOutput, calls=%fused_computation.7 | convolution fusion | flops 2476867584 | bytes 11268096 | tf_op jit(solution)/shard_map/dot_general | solution.py:136
  351.2 84.2 %reduce-scatter.2.cloned.1.call-done = bf16[192,768]{1,0:T(8,128)(2,1)} async-done(((bf16[3072,768]{1,0:T(8,128)(2,1)}), bf16[192,768]{1,0:T(8,128)(2,1)}) %reduce-scatter.2.cloned.1.call-update) | async-done | bytes 294928 | tf_op jit(solution)/shard_map/reduce_scatter | solution.py:135
  435.5 53.2 %all-reduce.7.cloned.1.call-done = bf16[192,768]{1,0:T(8,128)(2,1)} async-done(((bf16[192,768]{1,0:T(8,128)(2,1)}), bf16[192,768]{1,0:T(8,128)(2,1)}) %all-reduce.7.cloned.1.call-update) | async-done | bytes 294928 | tf_op jit(solution)/shard_map/psum | solution.py:143
  488.7 1.8 convert_element_type.139
  (36 shorter events, 0.6 us)
Async XLA Ops:
  7.2 66.1 %all-gather.7.cloned.1.call-start = ((), (), s32[]{:S(2)}) async-start(), calls=%async_computation.4 | async-start | bytes 5013504 | tf_op jit(solution)/shard_map/all_gather | solution.py:82
  9.3 113.4 %all-reduce.5.cloned.1.call-start = ((), (), s32[]{:S(2)}) async-start(), calls=%async_computation.1 | async-start | bytes 262144 | tf_op jit(solution)/shard_map/psum | solution.py:85
  38.2 35.1 %copy-start.6 = (bf16[3,64,768]{2,1,0:T(8,128)(2,1)S(1)}, bf16[3,64,768]{2,1,0:T(8,128)(2,1)}, u32[]{:S(2)}) copy-start(bf16[3,64,768]{2,1,0:T(8,128)(2,1)} %param.17) | copy-start | bytes 884740
  40.3 2.7 copy-start
  73.3 49.4 %copy-start.4 = (f32[1,256,128]{2,1,0:T(8,128)S(1)}, f32[1,256,128]{2,1,0:T(8,128)}, u32[]{:S(2)}) copy-start(f32[1,256,128]{2,1,0:T(8,128)} %param.10) | copy-start | bytes 393220
  73.3 50.4 %copy-start.3 = (bf16[3,64,3072]{2,1,0:T(8,128)(2,1)S(1)}, bf16[3,64,3072]{2,1,0:T(8,128)(2,1)}, u32[]{:S(2)}) copy-start(bf16[3,64,3072]{2,1,0:T(8,128)(2,1)} %param.14) | copy-start | bytes 3538948
  82.0 102.4 %all-gather.9.cloned.1.call-start = ((), (), s32[]{:S(2)}) async-start(), calls=%async_computation.5 | async-start | bytes 5013504 | tf_op jit(solution)/shard_map/all_gather | solution.py:97
  82.7 163.7 %all-gather.11.cloned.1.call-start = ((), (), s32[]{:S(2)}) async-start(), calls=%async_computation.6 | async-start | bytes 5013504 | tf_op jit(solution)/shard_map/all_gather | solution.py:96
  83.3 221.8 %all-reduce.9.cloned.1.call-start = ((), (), s32[]{:S(2)}) async-start(), calls=%async_computation.7 | async-start | bytes 393216 | tf_op jit(solution)/shard_map/psum | solution.py:117
  124.8 2.7 copy-start.2
  194.2 2.7 copy-start.1
  255.1 49.9 %copy-start.5 = (f32[256,128]{1,0:T(8,128)S(1)}, f32[256,128]{1,0:T(8,128)}, u32[]{:S(2)}) copy-start(f32[256,128]{1,0:T(8,128)} %all-reduce.5.cloned.1.call-done) | copy-start | bytes 393220
  264.0 171.5 %reduce-scatter.2.cloned.1.call-start = ((), (), s32[]{:S(2)}) async-start(), calls=%async_computation.2 | async-start | bytes 5013504 | tf_op jit(solution)/shard_map/reduce_scatter | solution.py:135
  351.2 137.5 %all-reduce.7.cloned.1.call-start = ((), (), s32[]{:S(2)}) async-start(), calls=%async_computation.3 | async-start | bytes 589824 | tf_op jit(solution)/shard_map/psum | solution.py:143
Sparse Core Ops, SparseCore 0:
  10.4 62.8 all-gather.6
  82.1 40.5 all-reduce.4
  125.4 58.9 all-gather.8
  187.6 58.7 all-gather.10
  264.1 40.9 all-reduce.8
  351.3 84.1 reduce-scatter.1
  438.1 50.5 all-reduce.6
where the time goes:
time: 499 us; the launch traced here: 497 us
  waiting for transfers between devices  353 us (71%)
  blocking collectives  54.2 us (11%)
  matrix products  49.3 us (10%)
  between operations  16.3 us (3%)
  local copies, waits for them, and re-layouts  13.7 us (3%)
  other arithmetic  10.1 us (2%)
    reduce_scatter x1, waiting for transfers between devices, body(): lax.psum_scatter(lax.dot_general(gen_hidden, upstream, (((0,), (0,)), (()...  84.2 us
    all_gather x1, waiting for transfers between devices, body(): lax.all_gather(proj_weight[2], 'fsdp', axis=0, tiled=True)  56.2 us
    psum x1, waiting for transfers between devices, body(): gen_grad = lax.psum(row_terms, 'dp').astype(jnp.float32)  53.2 us
    all_gather x1, waiting for transfers between devices, body(): lax.all_gather(proj_weight[1], 'fsdp', axis=0, tiled=True)  48.7 us
    psum x1, waiting for transfers between devices, body(): lax.psum(unembed_part(fake_cols + fake_part, unembed[2]).reshape(-1, 2 *...  41 us
    psum x1, waiting for transfers between devices, body(): clean_lat = lax.psum(clean_part, 'mp')  39.2 us
    psum x1, blocking collectives, body(): gap_total = lax.psum(jnp.sum(jnp.abs(clean_lat - real_pred)), 'fsdp')  34 us
    dot_general x4, matrix products, unembed_part(): lax.dot_general(residual_sum.astype(jnp.bfloat16), out_weight, (((1,), (1...  31.6 us
  transfers between devices with their start and end apart: 7, of which 7 were waited for; matrix products, arithmetic and copies ran while one was open for 5% of the time, Pallas kernels for 0%

commit v1 on v0

v1 whole, which is shorter than its diff:
```python
import math

import jax
import jax.numpy as jnp
from jax import lax
from jax.sharding import PartitionSpec as P

D = 3072
CH = 64
TEMB = 256


GUIDANCE = 3.5
EPS_NORM = 1e-06
EPS_GAP = 1e-05
HIGH = lax.Precision.HIGHEST


def sinusoid(timesteps):
    half_size = TEMB // 2
    frequency = jnp.exp(-math.log(10000.0) * jnp.arange(half_size, dtype=jnp.float32) / half_size)
    angles = timesteps.astype(jnp.float32)[:, None] * frequency[None, :]
    return jnp.concatenate([jnp.cos(angles), jnp.sin(angles)], axis=1)


def condition(timesteps, pooled):
    joined = jnp.concatenate([sinusoid(timesteps), pooled.astype(jnp.float32)], axis=1)
    return jax.nn.silu(joined).astype(jnp.bfloat16)


def mm(left, right):
    return jnp.dot(left, right, precision=HIGH, preferred_element_type=jnp.float32)


def doubled(block):
    zero = jnp.zeros_like(block)
    return jnp.concatenate(
        [jnp.concatenate([block, zero], axis=1), jnp.concatenate([zero, block], axis=1)], axis=0
    )


def body(
    gen_noise, renoise, gen_step, renoise_step, text_pooled, embed, mod_weight, proj_weight, unembed
):
    rows = proj_weight.shape[1]
    quarter = proj_weight.shape[2]
    fsdp_size = lax.axis_size("fsdp")
    row_start = lax.axis_index("fsdp") * rows
    col_start = lax.axis_index("mp") * quarter
    noisy_vec = condition(renoise_step, text_pooled)
    blank_vec = condition(renoise_step, jnp.zeros_like(text_pooled))
    gen_vec = condition(gen_step, text_pooled)
    teacher = jnp.dot(
        jnp.concatenate([noisy_vec, blank_vec], axis=0),
        mod_weight[1],
        preferred_element_type=jnp.float32,
    )
    local_mod = jnp.concatenate(
        [
            jnp.dot(gen_vec, mod_weight[0], preferred_element_type=jnp.float32),
            teacher[1:] + GUIDANCE * (teacher[:1] - teacher[1:]),
            jnp.dot(noisy_vec, mod_weight[2], preferred_element_type=jnp.float32),
        ],
        axis=0,
    )
    modulation = lax.all_gather(local_mod, "fsdp", axis=1, tiled=True)
    shift = lax.dynamic_slice_in_dim(modulation, row_start, rows, 1)
    gain = 1.0 + lax.dynamic_slice_in_dim(modulation, D + row_start, rows, 1)
    wide = embed.astype(jnp.float32)
    centred = wide - jnp.mean(wide, axis=2, keepdims=True)
    spread = jnp.einsum("mcd,med->mce", centred, centred, precision=HIGH) / D
    mine = lax.dynamic_slice_in_dim(centred, row_start, rows, 2)
    folded = jnp.einsum(
        "mrk,mok->mro", proj_weight, unembed, preferred_element_type=jnp.float32
    )
    maps = jnp.einsum("mcr,mro->mco", mine * gain[:, None, :], folded, precision=HIGH)
    offsets = jnp.einsum("mr,mro->mo", shift, folded, precision=HIGH)
    own_cols = lax.dynamic_slice_in_dim(embed, col_start, quarter, 2)
    direct = (
        jnp.einsum("mck,mok->mco", own_cols, unembed, preferred_element_type=jnp.float32)
        / fsdp_size
    )
    total = lax.psum(
        jnp.concatenate([maps, direct, offsets[:, None, :]], axis=1), ("fsdp", "mp")
    )
    maps, direct, offsets = total[:, :CH], total[:, CH : 2 * CH], total[:, 2 * CH :]

    halves = doubled(jnp.ones((CH, CH), jnp.float32))

    def inverse_std(values, which):
        energy = mm(values, doubled(spread[which])) * values
        return lax.rsqrt(jnp.maximum(mm(energy, halves), 0.0) + EPS_NORM)

    def predict(values, scale, which):
        offset = jnp.concatenate([offsets[which], offsets[which]], axis=1)
        return (
            mm(values, doubled(direct[which]))
            + scale * mm(values, doubled(maps[which]))
            + offset
        )

    latent = gen_noise[0].astype(jnp.bfloat16).astype(jnp.float32)
    gen_scale = inverse_std(latent, 0)
    clean_lat = predict(latent, gen_scale, 0)
    noise_level = renoise_step[0].astype(jnp.float32) / 1000.0
    noisy_lat = (1.0 - noise_level) * clean_lat + noise_level * renoise[0]
    noisy = noisy_lat.astype(jnp.bfloat16).astype(jnp.float32)
    real_out = predict(noisy, inverse_std(noisy, 1), 1)
    fake_out = predict(noisy, inverse_std(noisy, 2), 2)
    real_pred = noisy_lat - noise_level * real_out
    raw_gap = noise_level * (real_out - fake_out)
    moment = lax.dot_general(
        (gen_scale * latent).astype(jnp.bfloat16),
        raw_gap.astype(jnp.bfloat16),
        (((0,), (0,)), ((), ())),
        preferred_element_type=jnp.float32,
    )
    moment = moment[:CH, :CH] + moment[CH:, CH:]
    sums = jnp.sum(raw_gap, axis=0)
    sums = sums[:CH] + sums[CH:]
    distance = jnp.full((1, CH), jnp.sum(jnp.abs(clean_lat - real_pred)))
    reduced = lax.psum(jnp.concatenate([moment, sums[None], distance], axis=0), "fsdp")
    seq_len = 2 * gen_noise.shape[1] * fsdp_size
    gap_scale = reduced[CH + 1, 0] / (seq_len * CH) + EPS_GAP
    score_gap = raw_gap / gap_scale
    moment = reduced[: CH + 1] / (gap_scale * math.sqrt(seq_len * lax.axis_size("dp")))
    left = jnp.concatenate([mine[0] * gain[0][None], shift[:1]], axis=0)
    term = lax.dot_general(
        left, moment, (((0,), (0,)), ((), ())), precision=HIGH, preferred_element_type=jnp.float32
    )
    term = lax.psum(term, "dp")
    gen_grad = mm(term, unembed[0].astype(jnp.float32))
    return (gen_grad, score_gap[None])


def solution(mesh):
    return jax.shard_map(
        body,
        mesh=mesh,
        in_specs=(
            P("dp", "fsdp", None),
            P("dp", "fsdp", None),
            P("dp"),
            P("dp"),
            P("dp", None),
            P(),
            P(None, None, "fsdp"),
            P(None, "fsdp", "mp"),
            P(None, None, "mp"),
        ),
        out_specs=(P("fsdp", "mp"), P("dp", "fsdp", None)),
        check_vma=False,
    )
```

time: 499 us -> 650 us (1.30)
  the two profiles are of different devices: /device:TPU:1 before, /device:TPU:32 now
where the time goes in v1:
time: 650 us
  waiting for transfers between devices  492 us (76%)
  blocking collectives  116 us (18%)
  between operations  16.4 us (3%)
  matrix products  14.6 us (2%)
  other arithmetic  6.78 us (1%)
    psum x1, waiting for transfers between devices, body(): lax.psum(jnp.concatenate([maps, direct, offsets[:, None, :]], axis=1), ('...  492 us
    psum x1, blocking collectives, body(): lax.psum(jnp.concatenate([moment, sums[None], distance], axis=0), 'fsdp')  71.8 us
    all_gather x1, blocking collectives, body(): modulation = lax.all_gather(local_mod, 'fsdp', axis=1, tiled=True)  23.9 us
    psum x1, blocking collectives, body(): term = lax.psum(term, 'dp')  20.3 us
  transfers between devices with their start and end apart: 1, of which 1 were waited for; matrix products, arithmetic and copies ran while one was open for 1% of the time, Pallas kernels for 0%

profile of v1, /device:TPU:32, one launch (start us, length us, event | category | flops | bytes accessed | tf_op | source)
XLA Modules:
  0.0 649.7 jit_solution(15895108352038117610)
XLA Ops:
  7.2 0.8 convert_reduce_fusion.1
  8.1 0.7 convert_element_type.74
  10.3 1.3 fusion.14
  11.7 1.3 fusion.16
  13.1 1.3 fusion.18
  14.4 0.1 pad_maximum_fusion.1
  14.4 23.9 %all_gather.3 = f32[3,6144]{1,0:T(4,128)S(1)} all-gather(f32[3,384]{1,0:T(4,128)S(1)} %pad_maximum_fusion.1), channel_id=1, replica_groups=mesh['mp'=4,'fsdp'=16,'dp'=4] {'fsdp'}, dimensions={1}, use_global_device_ids=true | all-gather | bytes 78336 | tf_op jit(solution)/shard_map/all_gather | solution.py:66
  38.4 0.2 convert_reduce_fusion
  38.6 1.7 convert_subtract_fusion
  40.3 0.4 fusion.140
  40.8 0.2 convolution_multiply_fusion.5
  41.0 0.1 dynamic-slice_bitcast_fusion.1
  41.1 0.3 fusion.96
  41.4 1.4 fusion.24
  42.8 0.8 pad_maximum_fusion
  43.7 2.6 convolution_multiply_fusion.4
  46.3 1.0 fusion.66
  47.3 0.3 fusion.2
  47.6 0.3 fusion.4
  47.9 0.1 constant_dynamic-slice_fusion
  48.0 492.4 %all-reduce.20.cloned.1.call-done = f32[3,129,64]{1,2,0:T(8,128)} async-done(((f32[3,129,64]{1,2,0:T(8,128)}), f32[3,129,64]{1,2,0:T(8,128)}) %all-reduce.20.cloned.1.call-update) | async-done | bytes 99088 | tf_op jit(solution)/shard_map/psum | solution.py:83
  540.4 0.9 slice_reduce_fusion
  541.3 0.1 maximum_bitcast_fusion
  541.4 0.1 maximum_bitcast_fusion.1
  541.5 1.0 slice_bitcast_fusion.2
  542.5 0.3 fusion
  542.8 0.3 fusion.28
  543.1 0.3 convolution_multiply_fusion.3
  543.3 0.3 fusion.8
  543.6 0.1 maximum_bitcast_fusion.2
  543.7 0.3 convolution_multiply_fusion.1
  544.0 0.3 fusion.13
  544.2 0.3 convolution_multiply_fusion.2
  544.6 0.3 convolution_multiply_fusion
  544.9 0.9 abs_reduce_fusion
  545.8 0.3 fusion.139
  546.1 0.1 add_bitcast_fusion
  546.2 0.1 copy.17
  546.3 0.2 fusion.37
  546.5 0.1 slice_add_fusion
  546.6 0.7 pad.20.clone
  547.3 0.1 maximum_maximum_fusion
  547.4 71.8 %psum.22 = f32[66,64]{0,1:T(8,128)S(1)} all-reduce(f32[66,64]{0,1:T(8,128)S(1)} %maximum_maximum_fusion), channel_id=1, replica_groups=mesh['mp'=4,'fsdp'=16,'dp'=4] {'fsdp'}, use_global_device_ids=true, to_apply=%region_4.5 | all-reduce | flops 4224 | bytes 33792 | tf_op jit(solution)/shard_map/psum | solution.py:122
  619.1 0.6 slice.142
  620.4 0.7 divide_bitcast_fusion
  621.0 0.3 fusion.33
  621.4 20.3 %psum.23 = f32[192,64]{1,0:T(8,128)S(1)} all-reduce(f32[192,64]{1,0:T(8,128)S(1)} %fusion.33), channel_id=1, replica_groups=mesh['mp'=4,'fsdp'=16,'dp'=4] {'dp'}, use_global_device_ids=true, to_apply=%region_5.6 | all-reduce | flops 12288 | bytes 98304 | tf_op jit(solution)/shard_map/psum | solution.py:131
  641.7 1.2 fusion.29
  (28 shorter events, 0.4 us)
Async XLA Ops:
  7.2 33.2 %copy-start = (bf16[3,192,768]{2,1,0:T(8,128)(2,1)S(1)}, bf16[3,192,768]{2,1,0:T(8,128)(2,1)}, u32[]{:S(2)}) copy-start(bf16[3,192,768]{2,1,0:T(8,128)(2,1)} %param.16) | copy-start | bytes 2654212
  7.2 31.2 %copy-start.1 = (bf16[3,64,3072]{2,1,0:T(8,128)(2,1)S(1)}, bf16[3,64,3072]{2,1,0:T(8,128)(2,1)}, u32[]{:S(2)}) copy-start(bf16[3,64,3072]{2,1,0:T(8,128)(2,1)} %param.14) | copy-start | bytes 3538948
  7.2 533.2 %all-reduce.20.cloned.1.call-start = ((), (), s32[]{:S(2)}) async-start(), calls=%async_computation | async-start | bytes 393216 | tf_op jit(solution)/shard_map/psum | solution.py:83
  38.4 2.0 copy-start.2
  40.7 6.5 %copy-start.5 = (f32[1,256,128]{2,1,0:T(8,128)S(1)}, f32[1,256,128]{2,1,0:T(8,128)}, u32[]{:S(2)}) copy-start(f32[1,256,128]{2,1,0:T(8,128)} %param.9) | copy-start | bytes 393220
  41.0 6.6 %copy-start.3 = (f32[128,128]{1,0:T(8,128)S(1)}, f32[128,128]{1,0:T(8,128)}, u32[]{:S(2)}) copy-start(f32[128,128]{1,0:T(8,128)} %constant.68.clone.1) | copy-start | bytes 196612
  42.8 499.9 %copy-start.4 = (f32[1,256,128]{2,1,0:T(8,128)S(1)}, f32[1,256,128]{2,1,0:T(8,128)}, u32[]{:S(2)}) copy-start(f32[1,256,128]{2,1,0:T(8,128)} %param.10) | copy-start | bytes 393220
Sparse Core Ops, SparseCore 0:
  43.8 496.5 all-reduce.19

commit v2 on v1

v2 whole, which is shorter than its diff:
```python
import functools
import math

import jax
import jax.numpy as jnp
from jax import lax
from jax.experimental import pallas as pl
from jax.experimental.pallas import tpu as pltpu
from jax.sharding import PartitionSpec as P

D = 3072
CH = 64
TEMB = 256
TXT = 768

GUIDANCE = 3.5
EPS_NORM = 1e-06
EPS_GAP = 1e-05
HIGH = lax.Precision.HIGHEST
MESH = pl.DeviceIdType.MESH
F32 = jnp.float32
BF16 = jnp.bfloat16

MP = 4
DP = 4
NX = 4
NY = 4
SEQ = 8192
TOKENS = 32768
WIN = 384
ROWS = 192
HALF = 96
QUARTER = 768

S_MOD = 0
S_FOLD = 2
S_DIRECT = 5
S_X = 8
S_Y = 11
S_MAPS = 14
S_GEN = 17
S_SUM = 20
S_COL = 35
N_SEM = 50


def split3(values):
    high = values.astype(BF16)
    rest = values - high.astype(F32)
    mid = rest.astype(BF16)
    low = (rest - mid.astype(F32)).astype(BF16)
    return high, mid, low


def split2(values):
    high = values.astype(BF16)
    return high, (values - high.astype(F32)).astype(BF16)


def dot(left, right):
    return jnp.dot(left, right, preferred_element_type=F32)


def dot_nt(left, right):
    return lax.dot_general(left, right, (((1,), (1,)), ((), ())), preferred_element_type=F32)


def pack_pair(block):
    half = block.shape[0] // 2
    return jnp.concatenate([block[:half, :CH], block[half:, :CH]], axis=1)


def lanes(shape):
    return lax.broadcasted_iota(jnp.int32, shape, len(shape) - 1)


def sublanes(shape):
    return lax.broadcasted_iota(jnp.int32, shape, len(shape) - 2)


def doubled(packed):
    left = lanes(packed.shape) < CH
    turned = pltpu.roll(packed, CH, 1)
    zero = jnp.zeros_like(packed)
    return jnp.concatenate(
        [
            jnp.where(left, packed, zero),
            jnp.where(left, turned, zero),
            jnp.where(left, zero, turned),
            jnp.where(left, zero, packed),
        ],
        axis=0,
    )


def kernel(
    gen_noise, renoise, gen_step, renoise_step, text, embed, mod_weight, proj, unembed,
    grad_out, score_out,
    modw_v, proj_v, emb_v, une_v, noise_v, renoise_v, text_v,
    mod_send, mod_recv, fold_send, fold_recv, direct_v,
    x_send, x_recv, y_send, y_recv, maps_v, gen_v,
    mean_v, cov_v, scaled_v, left_v, sum_send, sum_recv, col_v,
    score_v, grad_v,
    load_sem, out_sem, send_sem, recv_sem,
):
    m = lax.axis_index("mp")
    f = lax.axis_index("fsdp")
    d = lax.axis_index("dp")
    y, x = lax.div(f, NX), lax.rem(f, NX)
    pair, side = lax.div(f, 2), lax.rem(f, 2)

    def load(src, dst, slot):
        copy = pltpu.make_async_copy(src, dst, load_sem.at[slot])
        copy.start()
        return copy

    ld_text = load(text, text_v, 0)
    ld_mod = [load(mod_weight.at[k], modw_v.at[k], 1 + k) for k in range(3)]
    ld_une = load(unembed, une_v, 4)
    ld_proj = load(proj, proj_v, 5)
    ld_emb = load(embed, emb_v, 6)
    ld_noise = load(gen_noise.at[0], noise_v, 7)
    ld_renoise = load(renoise.at[0], renoise_v, 8)

    def plane(dy, dx):
        return {"fsdp": lax.rem(y + dy, NY) * NX + lax.rem(x + dx, NX)}

    def column(dd, dm):
        return {"dp": lax.rem(d + dd, DP), "mp": lax.rem(m + dm, MP)}

    plane_steps = [(a, b) for a in range(NY) for b in range(NX) if a or b]
    column_steps = [(a, b) for a in range(DP) for b in range(MP) if a or b]

    barrier = pltpu.get_barrier_semaphore()
    for step in plane_steps:
        pl.semaphore_signal(barrier, inc=1, device_id=plane(*step), device_id_type=MESH)
    for step in column_steps:
        pl.semaphore_signal(barrier, inc=1, device_id=column(*step), device_id_type=MESH)

    def remote(src, dst, slot, device, recv_slot=None):
        return pltpu.make_async_remote_copy(
            src_ref=src,
            dst_ref=dst,
            send_sem=send_sem.at[slot],
            recv_sem=recv_sem.at[slot if recv_slot is None else recv_slot],
            device_id=device,
            device_id_type=MESH,
        )

    t_gen = gen_step[0].astype(F32)
    t_new = renoise_step[0].astype(F32)
    level = t_new / 1000.0
    lane = lanes((8, 128)).astype(F32)
    row8 = sublanes((8, 128))
    frequency = jnp.exp(-math.log(10000.0) * lane / 128)
    angles = jnp.where(row8 == 0, t_gen, t_new) * frequency
    waves = jnp.concatenate([jnp.cos(angles), jnp.sin(angles)], axis=1)
    ld_text.wait()
    words = jnp.broadcast_to(text_v[...].astype(F32), (8, TXT))
    words = jnp.where(sublanes((8, TXT)) < 2, words, 0.0)
    joined = jnp.concatenate([waves, words], axis=1)
    joined = joined / (1.0 + jnp.exp(-joined))
    vectors = jnp.concatenate([joined, jnp.zeros_like(joined)], axis=0).astype(BF16)

    ld_mod[0].wait()
    out0 = dot(vectors, modw_v[0])
    ld_mod[1].wait()
    out1 = dot(vectors, modw_v[1])
    ld_mod[2].wait()
    out2 = dot(vectors, modw_v[2])
    guided = out1[2:3] + GUIDANCE * (out1[1:2] - out1[2:3])
    rows = sublanes((8, WIN))
    mod_send[...] = jnp.where(
        rows == 0, out0[0:1], jnp.where(rows == 1, guided, jnp.where(rows == 2, out2[1:2], 0.0))
    )

    pl.semaphore_wait(barrier, len(plane_steps) + len(column_steps))

    kind = lax.div(f, 8)
    first = 2 * lax.rem(f, 8)

    def mod_copy(k):
        return remote(
            mod_send, mod_recv.at[kind], S_MOD + k, {"fsdp": first + k}, recv_slot=S_MOD + kind
        )

    for k in range(2):
        @pl.when(first + k != f)
        def _():
            mod_copy(k).start()

    @pl.when(f == 0)
    def _():
        mod_recv[0] = mod_send[...]

    @pl.when(f == NX * NY - 1)
    def _():
        mod_recv[1] = mod_send[...]

    ld_une.wait()
    ld_proj.wait()
    for k in range(3):
        fold_send[k] = pack_pair(dot_nt(proj_v[k], une_v[k]))
    ld_emb.wait()
    for k in range(3):
        own = emb_v[k, :, pl.ds(pl.multiple_of(m * QUARTER, 128), QUARTER)]
        fold_send[3, 32 * k : 32 * k + 32, :] = pack_pair(dot_nt(own, une_v[k]))
    fold_copies = []
    for r in range(1, MP):
        target = lax.rem(m + r, MP)
        copy = remote(fold_send.at[target], fold_recv.at[r - 1], S_FOLD + r - 1, {"mp": target})
        copy.start()
        fold_copies.append(copy)

    for k in range(3):
        mean_v[k] = jnp.broadcast_to(
            jnp.mean(emb_v[k].astype(F32), axis=1, keepdims=True), (CH, 128)
        )

    def covariance(k):
        centred = emb_v[k].astype(F32) - mean_v[k][:, :1]
        parts = jnp.concatenate(split3(centred), axis=0)
        gram = dot_nt(parts, parts)
        gram = gram[:CH] + gram[CH : 2 * CH] + gram[2 * CH :]
        gram = (gram[:, :CH] + gram[:, CH : 2 * CH] + gram[:, 2 * CH :]) * (1.0 / D)
        cov_v[k] = jnp.concatenate(split3(doubled(pack_pair(gram))), axis=0)

    covariance(0)

    for copy in fold_copies:
        copy.wait_recv()
    folded = fold_send[m] + fold_recv[0] + fold_recv[1] + fold_recv[2]

    def direct_copy(r):
        return remote(direct_v, direct_v, S_DIRECT + r, {"mp": r}, recv_slot=S_DIRECT)

    @pl.when(m == MP - 1)
    def _():
        direct_v[...] = folded
        for r in range(MP - 1):
            direct_copy(r).start()

    @pl.when(f != 0)
    def _():
        remote(mod_send, mod_recv.at[0], S_MOD, {"fsdp": first}).wait_recv()

    @pl.when(f != NX * NY - 1)
    def _():
        remote(mod_send, mod_recv.at[1], S_MOD + 1, {"fsdp": first}).wait_recv()

    gen_v[d] = jnp.where(
        rows == 0, mod_recv[0, 0:1, :], jnp.where(rows == 1, mod_recv[1, 0:1, :], 0.0)
    )
    gen_copies = []
    for r in range(1, DP):
        copy = remote(gen_v.at[d], gen_v.at[d], S_GEN + r - 1, {"dp": lax.rem(d + r, DP)})
        copy.start()
        gen_copies.append(copy)

    model = jnp.minimum(m, 2)
    window = pl.ds(pl.multiple_of(pair * WIN, 128), WIN)
    shift = mod_recv[0, pl.ds(m, 1), :]
    gain = 1.0 + mod_recv[1, pl.ds(m, 1), :]
    centred = emb_v[model, :, window].astype(F32) - mean_v[model][:, :1]
    left = jnp.concatenate([centred * gain, jnp.broadcast_to(shift, (8, WIN))], axis=0)
    weight = jnp.concatenate([folded[:, :CH], folded[:, CH:]], axis=0)
    none = jnp.zeros_like(weight)
    weight = jnp.concatenate(
        [jnp.where(side == 0, weight, none), jnp.where(side == 0, none, weight)], axis=0
    )
    result = jnp.dot(left, weight, precision=HIGH, preferred_element_type=F32)
    x_send[0:32, :] = pack_pair(result[:CH])
    x_send[32:40, :] = jnp.concatenate([result[CH:], result[CH:]], axis=1)

    x_copies = []
    for r in range(1, NX):
        copy = remote(x_send, x_recv.at[r - 1], S_X + r - 1, plane(0, r))
        copy.start()
        x_copies.append(copy)
    covariance(1)
    for copy in x_copies:
        copy.wait_recv()
    y_send[...] = x_send[...] + x_recv[0] + x_recv[1] + x_recv[2]
    y_copies = []
    for r in range(1, NY):
        copy = remote(y_send, y_recv.at[r - 1], S_Y + r - 1, plane(r, 0))
        copy.start()
        y_copies.append(copy)
    covariance(2)
    for copy in y_copies:
        copy.wait_recv()
    maps_v[m] = y_send[...] + y_recv[0] + y_recv[1] + y_recv[2]
    map_copies = []
    for r in range(1, MP):
        copy = remote(maps_v.at[m], maps_v.at[m], S_MAPS + r - 1, {"mp": lax.rem(m + r, MP)})
        copy.start()
        map_copies.append(copy)

    ones = jnp.where(
        (lanes((128, 128)) < CH) == (sublanes((128, 128)) < CH), 1.0, 0.0
    ).astype(BF16)
    ones = jnp.concatenate([ones, ones, ones], axis=0)

    def inverse_std(values, k):
        thrice = jnp.concatenate([values, values, values], axis=1)
        energy = dot(thrice, cov_v[k]) * values.astype(F32)
        energy = jnp.concatenate(split3(energy), axis=1)
        return lax.rsqrt(jnp.maximum(dot(energy, ones), 0.0) + EPS_NORM)

    def stacked(packed):
        return jnp.concatenate(split2(doubled(packed)), axis=0)

    ld_noise.wait()
    latent = noise_v[...].astype(BF16)
    gen_scale = inverse_std(latent, 0)
    scaled_v[...] = jnp.transpose(latent.astype(F32) * gen_scale).astype(BF16)
    twice = jnp.concatenate([latent, latent], axis=1)

    @pl.when(m != MP - 1)
    def _():
        remote(direct_v, direct_v, S_DIRECT, {"mp": MP - 1}).wait_recv()

    gen_direct = dot(twice, stacked(direct_v[0:32, :]))
    ld_renoise.wait()

    for copy in map_copies:
        copy.wait_recv()
    clean = (
        gen_direct + gen_scale * dot(twice, stacked(maps_v[0, 0:32, :])) + maps_v[0, 32:33, :]
    )
    noisy = (1.0 - level) * clean + level * renoise_v[...]
    values = noisy.astype(BF16)
    twice = jnp.concatenate([values, values], axis=1)
    weights = jnp.concatenate(
        [
            stacked(direct_v[32:64, :]),
            stacked(maps_v[1, 0:32, :]),
            stacked(direct_v[64:96, :]),
            stacked(maps_v[2, 0:32, :]),
        ],
        axis=1,
    )
    products = dot(twice, weights)
    real = products[:, :128] + inverse_std(values, 1) * products[:, 128:256] + maps_v[1, 32:33, :]
    fake = products[:, 256:384] + inverse_std(values, 2) * products[:, 384:] + maps_v[2, 32:33, :]
    gap = level * (real - fake)
    distance = jnp.abs(clean - noisy + level * real)

    moment = dot(scaled_v[...], gap.astype(BF16))
    moment = moment[:CH] + pltpu.roll(moment[CH:], CH, 1)
    left32 = lanes((32, 128)) < CH
    moment = jnp.where(left32, moment[:32], pltpu.roll(moment[32:], CH, 1))
    piece = moment[0:8]
    for k in range(1, MP):
        piece = jnp.where(m == k, moment[8 * k : 8 * k + 8], piece)
    total = jnp.sum(gap, axis=0, keepdims=True)
    total = total + pltpu.roll(total, CH, 1)
    spread = jnp.sum(distance, axis=0, keepdims=True)
    sum_send[0:8, :] = piece
    sum_send[8:16, :] = jnp.where(row8 == 0, total, jnp.where(row8 == 1, spread, 0.0))
    sum_copies = []
    for k, step in enumerate(plane_steps):
        copy = remote(sum_send, sum_recv.at[k], S_SUM + k, plane(*step))
        copy.start()
        sum_copies.append(copy)

    for copy in gen_copies:
        copy.wait_recv()
    centred = emb_v[0, :, window].astype(F32) - mean_v[0][:, :1]
    pieces = [centred[:32] * (1.0 + gen_v[s, 1:2, :]) for s in range(DP)]
    pieces += [centred[32:] * (1.0 + gen_v[s, 1:2, :]) for s in range(DP)]
    pieces += [jnp.where(rows == 0, gen_v[s], 0.0) for s in range(DP)]
    pieces += [jnp.zeros((96, WIN), F32)]
    left_v[...] = jnp.transpose(jnp.concatenate(pieces, axis=0)).astype(BF16)

    for copy in sum_copies:
        copy.wait_recv()
    sums = sum_send[...]
    for k in range(len(plane_steps)):
        sums = sums + sum_recv[k]
    gap_scale = jnp.sum(sums[9:10, :], axis=1, keepdims=True) / (SEQ * CH) + EPS_GAP
    slot = d * MP + m
    col_v[slot] = (sums / (gap_scale * math.sqrt(TOKENS))).astype(BF16)
    col_copies = []
    for k, step in enumerate(column_steps):
        copy = remote(col_v.at[slot], col_v.at[slot], S_COL + k, column(*step))
        copy.start()
        col_copies.append(copy)
    score_v[...] = gap / gap_scale
    score_copy = pltpu.make_async_copy(score_v, score_out.at[0], out_sem.at[0])
    score_copy.start()

    for copy in col_copies:
        copy.wait_recv()
    table = [col_v[k].astype(F32) for k in range(DP * MP)]
    block = jnp.concatenate([entry[:8] for entry in table], axis=0)
    right = jnp.concatenate(
        [block, pltpu.roll(block, CH, 1)]
        + [table[MP * s][8:] for s in range(DP)]
        + [jnp.zeros((96, 128), F32)],
        axis=0,
    ).astype(BF16)
    own_rows = left_v[pl.ds(pl.multiple_of(side * ROWS, 64), ROWS), :]
    term = dot(own_rows, right)[:, :CH].astype(BF16)
    grad_v[...] = dot(term, une_v[0])
    grad_copy = pltpu.make_async_copy(grad_v, grad_out, out_sem.at[1])
    grad_copy.start()

    for k in range(2):
        @pl.when(first + k != f)
        def _():
            mod_copy(k).wait_send()

    @pl.when(m == MP - 1)
    def _():
        for r in range(MP - 1):
            direct_copy(r).wait_send()

    for copy in (
        fold_copies + x_copies + y_copies + map_copies + gen_copies + sum_copies + col_copies
    ):
        copy.wait_send()
    score_copy.wait()
    grad_copy.wait()


def body(
    gen_noise, renoise, gen_step, renoise_step, text_pooled, embed, mod_weight, proj_weight, unembed
):
    hbm = pl.BlockSpec(memory_space=pl.ANY)
    smem = pl.BlockSpec(memory_space=pltpu.SMEM)
    vmem = pltpu.VMEM
    return pl.pallas_call(
        kernel,
        out_shape=(
            jax.ShapeDtypeStruct((ROWS, QUARTER), F32),
            jax.ShapeDtypeStruct(gen_noise.shape, F32),
        ),
        in_specs=[hbm, hbm, smem, smem, hbm, hbm, hbm, hbm, hbm],
        out_specs=(hbm, hbm),
        scratch_shapes=[
            vmem((3, TEMB + TXT, WIN), BF16),
            vmem((3, ROWS, QUARTER), BF16),
            vmem((3, CH, D), BF16),
            vmem((3, CH, QUARTER), BF16),
            vmem((256, 128), F32),
            vmem((256, 128), F32),
            vmem((1, TXT), BF16),
            vmem((8, WIN), F32),
            vmem((2, 8, WIN), F32),
            vmem((4, HALF, 128), F32),
            vmem((3, HALF, 128), F32),
            vmem((HALF, 128), F32),
            vmem((40, 128), F32),
            vmem((3, 40, 128), F32),
            vmem((40, 128), F32),
            vmem((3, 40, 128), F32),
            vmem((4, 40, 128), F32),
            vmem((DP, 8, WIN), F32),
            vmem((3, CH, 128), F32),
            vmem((3, 384, 128), BF16),
            vmem((128, 256), BF16),
            vmem((WIN, 384), BF16),
            vmem((16, 128), F32),
            vmem((15, 16, 128), F32),
            vmem((16, 16, 128), BF16),
            vmem((256, 128), F32),
            vmem((ROWS, QUARTER), F32),
            pltpu.SemaphoreType.DMA((9,)),
            pltpu.SemaphoreType.DMA((2,)),
            pltpu.SemaphoreType.DMA((N_SEM,)),
            pltpu.SemaphoreType.DMA((N_SEM,)),
        ],
        compiler_params=pltpu.CompilerParams(collective_id=0, has_side_effects=True),
        name="distill",
    )(
        gen_noise, renoise, gen_step, renoise_step, text_pooled, embed, mod_weight, proj_weight,
        unembed,
    )


def solution(mesh):
    return jax.shard_map(
        body,
        mesh=mesh,
        in_specs=(
            P("dp", "fsdp", None),
            P("dp", "fsdp", None),
            P("dp"),
            P("dp"),
            P("dp", None),
            P(),
            P(None, None, "fsdp"),
            P(None, "fsdp", "mp"),
            P(None, None, "mp"),
        ),
        out_specs=(P("fsdp", "mp"), P("dp", "fsdp", None)),
        check_vma=False,
    )
```

time: 650 us -> 45.4 us (0.07)
  the two profiles are of different devices: /device:TPU:32 before, /device:TPU:1 now
where the time goes in v2:
time: 45.4 us; the launch traced here: 45.2 us
  Pallas kernels  39.8 us (88%)
  local copies, waits for them, and re-layouts  3.48 us (8%)
  between operations  1.93 us (4%)
    pallas_call x1, Pallas kernels, body(): pl.pallas_call(kernel, out_shape=(jax.ShapeDtypeStruct((ROWS, QUARTER), F...  39.8 us
    unnamed x2, local copies, waits for them, and re-layouts  3.48 us

profile of v2, /device:TPU:1, one launch (start us, length us, event | category | flops | bytes accessed | tf_op | source)
XLA Modules:
  0.0 45.2 jit_solution(613702517552605723)
XLA Ops:
  1.9 39.8 %distill.1 = (f32[192,768]{1,0:T(8,128)}, f32[1,256,128]{2,1,0:T(8,128)}) custom-call(f32[1,256,128]{2,1,0:T(8,128)} %gen_noise.1, f32[1,256,128]{2,1,0:T(8,128)} %renoise.1, s32[1]{0:T(128)S(6)} %copy.13.gen_step, s32[1]{0:T(128)S(6)} %copy.14.renoise_step, bf16[1,768]{1,0:T(2,128)(2,1)} %text.1, bf16[3,64,3072]{2,1,0:T(8,128)(2,1)} %embed.1, ...), custom_call_target="tpu_custom_call" | custom-call | tf_op jit(solution)/shard_map/distill/pallas_call | solution.py:433
  41.7 1.9 %copy.15 = f32[192,768]{1,0:T(8,128)} copy(f32[192,768]{1,0:T(8,128)} %get-tuple-element.4) | data formatting | bytes 1179648
  43.7 1.6 %copy.16 = f32[1,256,128]{2,1,0:T(8,128)} copy(f32[1,256,128]{2,1,0:T(8,128)} %get-tuple-element.5) | data formatting | bytes 262144

commit v3 on v2

--- a/solution.py
+++ b/solution.py
@@ -68,6 +68,17 @@
 def pack_pair(block):
     half = block.shape[0] // 2
     return jnp.concatenate([block[:half, :CH], block[half:, :CH]], axis=1)
+
+
+def rounded_map(packed, shift):
+    return jnp.concatenate([packed.astype(BF16), *split2(shift)], axis=0)
+
+
+def summed_map(own, received):
+    total = own[...].astype(F32)
+    for k in range(3):
+        total = total + received[k].astype(F32)
+    return rounded_map(total[:32], total[32:40] + total[40:48])
 
 
 def lanes(shape):
@@ -95,12 +106,12 @@
 
 def kernel(
     gen_noise, renoise, gen_step, renoise_step, text, embed, mod_weight, proj, unembed,
-    grad_out, score_out,
+    term_out, score_out,
     modw_v, proj_v, emb_v, une_v, noise_v, renoise_v, text_v,
     mod_send, mod_recv, fold_send, fold_recv, direct_v,
     x_send, x_recv, y_send, y_recv, maps_v, gen_v,
     mean_v, cov_v, scaled_v, left_v, sum_send, sum_recv, col_v,
-    score_v, grad_v,
+    score_v, term_v, weight_v, centre_v, direct_w,
     load_sem, out_sem, send_sem, recv_sem,
 ):
     m = lax.axis_index("mp")
@@ -128,8 +139,11 @@
     def column(dd, dm):
         return {"dp": lax.rem(d + dd, DP), "mp": lax.rem(m + dm, MP)}
 
-    plane_steps = [(a, b) for a in range(NY) for b in range(NX) if a or b]
-    column_steps = [(a, b) for a in range(DP) for b in range(MP) if a or b]
+    def farthest_first(steps):
+        return sorted(steps, key=lambda step: -sum(min(n, 4 - n) for n in step))
+
+    plane_steps = farthest_first([(a, b) for a in range(NY) for b in range(NX) if a or b])
+    column_steps = farthest_first([(a, b) for a in range(DP) for b in range(MP) if a or b])
 
     barrier = pltpu.get_barrier_semaphore()
     for step in plane_steps:
@@ -240,47 +254,53 @@
         for r in range(MP - 1):
             direct_copy(r).start()
 
-    @pl.when(f != 0)
-    def _():
-        remote(mod_send, mod_recv.at[0], S_MOD, {"fsdp": first}).wait_recv()
-
-    @pl.when(f != NX * NY - 1)
-    def _():
-        remote(mod_send, mod_recv.at[1], S_MOD + 1, {"fsdp": first}).wait_recv()
-
-    gen_v[d] = jnp.where(
-        rows == 0, mod_recv[0, 0:1, :], jnp.where(rows == 1, mod_recv[1, 0:1, :], 0.0)
-    )
-    gen_copies = []
-    for r in range(1, DP):
-        copy = remote(gen_v.at[d], gen_v.at[d], S_GEN + r - 1, {"dp": lax.rem(d + r, DP)})
-        copy.start()
-        gen_copies.append(copy)
-
     model = jnp.minimum(m, 2)
     window = pl.ds(pl.multiple_of(pair * WIN, 128), WIN)
-    shift = mod_recv[0, pl.ds(m, 1), :]
-    gain = 1.0 + mod_recv[1, pl.ds(m, 1), :]
-    centred = emb_v[model, :, window].astype(F32) - mean_v[model][:, :1]
-    left = jnp.concatenate([centred * gain, jnp.broadcast_to(shift, (8, WIN))], axis=0)
+    centre_v[...] = emb_v[model, :, window].astype(F32) - mean_v[model][:, :1]
     weight = jnp.concatenate([folded[:, :CH], folded[:, CH:]], axis=0)
     none = jnp.zeros_like(weight)
     weight = jnp.concatenate(
         [jnp.where(side == 0, weight, none), jnp.where(side == 0, none, weight)], axis=0
     )
-    result = jnp.dot(left, weight, precision=HIGH, preferred_element_type=F32)
-    x_send[0:32, :] = pack_pair(result[:CH])
-    x_send[32:40, :] = jnp.concatenate([result[CH:], result[CH:]], axis=1)
+    high, low = split2(weight)
+    weight_v[...] = jnp.concatenate([high, low, high], axis=0)
+
+    @pl.when(f != 0)
+    def _():
+        remote(mod_send, mod_recv.at[0], S_MOD, {"fsdp": first}).wait_recv()
+
+    @pl.when(f != NX * NY - 1)
+    def _():
+        remote(mod_send, mod_recv.at[1], S_MOD + 1, {"fsdp": first}).wait_recv()
+
+    shift = mod_recv[0, pl.ds(m, 1), :]
+    gain = 1.0 + mod_recv[1, pl.ds(m, 1), :]
+    left = jnp.concatenate([centre_v[...] * gain, jnp.broadcast_to(shift, (8, WIN))], axis=0)
+    high, low = split2(left)
+    result = dot(jnp.concatenate([high, high, low], axis=1), weight_v[...])
+    x_send[...] = rounded_map(
+        pack_pair(result[:CH]), jnp.concatenate([result[CH:], result[CH:]], axis=1)
+    )
 
     x_copies = []
     for r in range(1, NX):
         copy = remote(x_send, x_recv.at[r - 1], S_X + r - 1, plane(0, r))
         copy.start()
         x_copies.append(copy)
+
+    gen_v[d] = jnp.where(
+        rows == 0, mod_recv[0, 0:1, :], jnp.where(rows == 1, mod_recv[1, 0:1, :], 0.0)
+    )
+    gen_copies = []
+    for r in range(1, DP):
+        copy = remote(gen_v.at[d], gen_v.at[d], S_GEN + r - 1, {"dp": lax.rem(d + r, DP)})
+        copy.start()
+        gen_copies.append(copy)
+
     covariance(1)
     for copy in x_copies:
         copy.wait_recv()
-    y_send[...] = x_send[...] + x_recv[0] + x_recv[1] + x_recv[2]
+    y_send[...] = summed_map(x_send, x_recv)
     y_copies = []
     for r in range(1, NY):
         copy = remote(y_send, y_recv.at[r - 1], S_Y + r - 1, plane(r, 0))
@@ -289,7 +309,7 @@
     covariance(2)
     for copy in y_copies:
         copy.wait_recv()
-    maps_v[m] = y_send[...] + y_recv[0] + y_recv[1] + y_recv[2]
+    maps_v[m] = summed_map(y_send, y_recv)
     map_copies = []
     for r in range(1, MP):
         copy = remote(maps_v.at[m], maps_v.at[m], S_MAPS + r - 1, {"mp": lax.rem(m + r, MP)})
@@ -321,28 +341,28 @@
         remote(direct_v, direct_v, S_DIRECT, {"mp": MP - 1}).wait_recv()
 
     gen_direct = dot(twice, stacked(direct_v[0:32, :]))
+    direct_w[:, :128] = stacked(direct_v[32:64, :])
+    direct_w[:, 128:] = stacked(direct_v[64:96, :])
     ld_renoise.wait()
 
     for copy in map_copies:
         copy.wait_recv()
-    clean = (
-        gen_direct + gen_scale * dot(twice, stacked(maps_v[0, 0:32, :])) + maps_v[0, 32:33, :]
-    )
+
+    def map_of(k):
+        return doubled(maps_v[k, 0:32, :].astype(F32)).astype(BF16)
+
+    def shift_of(k):
+        rows16 = maps_v[k, 32:48, :].astype(F32)
+        return rows16[0:1] + rows16[8:9]
+
+    clean = gen_direct + gen_scale * dot(latent, map_of(0)) + shift_of(0)
     noisy = (1.0 - level) * clean + level * renoise_v[...]
     values = noisy.astype(BF16)
     twice = jnp.concatenate([values, values], axis=1)
-    weights = jnp.concatenate(
-        [
-            stacked(direct_v[32:64, :]),
-            stacked(maps_v[1, 0:32, :]),
-            stacked(direct_v[64:96, :]),
-            stacked(maps_v[2, 0:32, :]),
-        ],
-        axis=1,
-    )
-    products = dot(twice, weights)
-    real = products[:, :128] + inverse_std(values, 1) * products[:, 128:256] + maps_v[1, 32:33, :]
-    fake = products[:, 256:384] + inverse_std(values, 2) * products[:, 384:] + maps_v[2, 32:33, :]
+    direct = dot(twice, direct_w[...])
+    mapped = dot(values, jnp.concatenate([map_of(1), map_of(2)], axis=1))
+    real = direct[:, :128] + inverse_std(values, 1) * mapped[:, :128] + shift_of(1)
+    fake = direct[:, 128:] + inverse_std(values, 2) * mapped[:, 128:] + shift_of(2)
     gap = level * (real - fake)
     distance = jnp.abs(clean - noisy + level * real)
 
@@ -356,8 +376,14 @@
     total = jnp.sum(gap, axis=0, keepdims=True)
     total = total + pltpu.roll(total, CH, 1)
     spread = jnp.sum(distance, axis=0, keepdims=True)
-    sum_send[0:8, :] = piece
-    sum_send[8:16, :] = jnp.where(row8 == 0, total, jnp.where(row8 == 1, spread, 0.0))
+    tail = []
+    for term in split2(total) + split2(spread):
+        tail.append(jnp.broadcast_to(term.astype(F32), (8, 128)))
+    tail = jnp.where(
+        row8 == 0, tail[0], jnp.where(row8 == 1, tail[1], jnp.where(row8 == 2, tail[2], tail[3]))
+    )
+    tail = jnp.where(row8 < 4, tail, 0.0)
+    sum_send[...] = jnp.concatenate([piece, tail], axis=0).astype(BF16)
     sum_copies = []
     for k, step in enumerate(plane_steps):
         copy = remote(sum_send, sum_recv.at[k], S_SUM + k, plane(*step))
@@ -375,10 +401,13 @@
 
     for copy in sum_copies:
         copy.wait_recv()
-    sums = sum_send[...]
+    sums = sum_send[...].astype(F32)
     for k in range(len(plane_steps)):
-        sums = sums + sum_recv[k]
-    gap_scale = jnp.sum(sums[9:10, :], axis=1, keepdims=True) / (SEQ * CH) + EPS_GAP
+        sums = sums + sum_recv[k].astype(F32)
+    spread = sums[10:11, :] + sums[11:12, :]
+    gap_scale = jnp.sum(spread, axis=1, keepdims=True) / (SEQ * CH) + EPS_GAP
+    total = jnp.where(row8 == 0, sums[8:9, :] + sums[9:10, :], 0.0)
+    sums = jnp.concatenate([sums[0:8], total], axis=0)
     slot = d * MP + m
     col_v[slot] = (sums / (gap_scale * math.sqrt(TOKENS))).astype(BF16)
     col_copies = []
@@ -401,10 +430,9 @@
         axis=0,
     ).astype(BF16)
     own_rows = left_v[pl.ds(pl.multiple_of(side * ROWS, 64), ROWS), :]
-    term = dot(own_rows, right)[:, :CH].astype(BF16)
-    grad_v[...] = dot(term, une_v[0])
-    grad_copy = pltpu.make_async_copy(grad_v, grad_out, out_sem.at[1])
-    grad_copy.start()
+    term_v[...] = dot(own_rows, right).astype(BF16)
+    term_copy = pltpu.make_async_copy(term_v, term_out, out_sem.at[1])
+    term_copy.start()
 
     for k in range(2):
         @pl.when(first + k != f)
@@ -421,7 +449,35 @@
     ):
         copy.wait_send()
     score_copy.wait()
-    grad_copy.wait()
+    term_copy.wait()
+
+
+def finish(
+    term, unembed, score, grad_out, score_out, term_v, une_v, score_v, grad_v, in_sem, out_sem
+):
+    loads = [
+        pltpu.make_async_copy(src, dst, in_sem.at[k])
+        for k, (src, dst) in enumerate(
+            [(term, term_v), (unembed.at[0], une_v), (score.at[0], score_v)]
+        )
+    ]
+    for copy in loads:
+        copy.start()
+    loads[0].wait()
+    loads[1].wait()
+    stores = []
+    for k in range(2):
+        rows = slice(HALF * k, HALF * k + HALF)
+        grad_v[rows, :] = dot(term_v[rows, :CH], une_v[...])
+        copy = pltpu.make_async_copy(grad_v.at[rows], grad_out.at[rows], out_sem.at[k])
+        copy.start()
+        stores.append(copy)
+    loads[2].wait()
+    copy = pltpu.make_async_copy(score_v, score_out.at[0], out_sem.at[2])
+    copy.start()
+    stores.append(copy)
+    for copy in stores:
+        copy.wait()
 
 
 def body(
@@ -430,10 +486,10 @@
     hbm = pl.BlockSpec(memory_space=pl.ANY)
     smem = pl.BlockSpec(memory_space=pltpu.SMEM)
     vmem = pltpu.VMEM
-    return pl.pallas_call(
+    term, score = pl.pallas_call(
         kernel,
         out_shape=(
-            jax.ShapeDtypeStruct((ROWS, QUARTER), F32),
+            jax.ShapeDtypeStruct((ROWS, 128), BF16),
             jax.ShapeDtypeStruct(gen_noise.shape, F32),
         ),
         in_specs=[hbm, hbm, smem, smem, hbm, hbm, hbm, hbm, hbm],
@@ -451,21 +507,24 @@
             vmem((4, HALF, 128), F32),
             vmem((3, HALF, 128), F32),
             vmem((HALF, 128), F32),
-            vmem((40, 128), F32),
-            vmem((3, 40, 128), F32),
-            vmem((40, 128), F32),
-            vmem((3, 40, 128), F32),
-            vmem((4, 40, 128), F32),
+            vmem((48, 128), BF16),
+            vmem((3, 48, 128), BF16),
+            vmem((48, 128), BF16),
+            vmem((3, 48, 128), BF16),
+            vmem((4, 48, 128), BF16),
             vmem((DP, 8, WIN), F32),
             vmem((3, CH, 128), F32),
             vmem((3, 384, 128), BF16),
             vmem((128, 256), BF16),
             vmem((WIN, 384), BF16),
-            vmem((16, 128), F32),
-            vmem((15, 16, 128), F32),
+            vmem((16, 128), BF16),
+            vmem((15, 16, 128), BF16),
             vmem((16, 16, 128), BF16),
             vmem((256, 128), F32),
-            vmem((ROWS, QUARTER), F32),
+            vmem((ROWS, 128), BF16),
+            vmem((3 * WIN, CH), BF16),
+            vmem((CH, WIN), F32),
+            vmem((256, 256), BF16),
             pltpu.SemaphoreType.DMA((9,)),
             pltpu.SemaphoreType.DMA((2,)),
             pltpu.SemaphoreType.DMA((N_SEM,)),
@@ -477,6 +536,24 @@
         gen_noise, renoise, gen_step, renoise_step, text_pooled, embed, mod_weight, proj_weight,
         unembed,
     )
+    return pl.pallas_call(
+        finish,
+        out_shape=(
+            jax.ShapeDtypeStruct((ROWS, QUARTER), F32),
+            jax.ShapeDtypeStruct(gen_noise.shape, F32),
+        ),
+        in_specs=[hbm, hbm, hbm],
+        out_specs=(hbm, hbm),
+        scratch_shapes=[
+            vmem((ROWS, 128), BF16),
+            vmem((CH, QUARTER), BF16),
+            vmem((256, 128), F32),
+            vmem((ROWS, QUARTER), F32),
+            pltpu.SemaphoreType.DMA((3,)),
+            pltpu.SemaphoreType.DMA((3,)),
+        ],
+        name="finish",
+    )(term, unembed, score)
 
 
 def solution(mesh):

time: 45.4 us -> 41.5 us (0.914)
  local copies, waits for them, and re-layouts: 3.48 us -> 0 us
    unnamed x2 -> x0, local copies, waits for them, and re-layouts: 3.48 us -> none
    pallas_call x1 -> x2, Pallas kernels: 39.8 us -> 39.4 us  [the longest x1 37.4 us: body(): pl.pallas_call(kernel, out_shape=(jax.ShapeDtypeStruct((ROWS, 128), BF16)...]
where the time goes in v3:
time: 41.5 us; the launch traced here: 41.4 us
  Pallas kernels  39.4 us (95%)
  between operations  1.93 us (5%)
    pallas_call x1, Pallas kernels, body(): pl.pallas_call(kernel, out_shape=(jax.ShapeDtypeStruct((ROWS, 128), BF16)...  37.4 us
    pallas_call x1, Pallas kernels, body(): pl.pallas_call(finish, out_shape=(jax.ShapeDtypeStruct((ROWS, QUARTER), F...  2 us

profile of v3, /device:TPU:1, one launch (start us, length us, event | category | flops | bytes accessed | tf_op | source)
XLA Modules:
  0.0 41.4 jit_solution(16749498491703677506)
XLA Ops:
  1.9 37.4 %distill.1 = (bf16[192,128]{1,0:T(8,128)(2,1)}, f32[1,256,128]{2,1,0:T(8,128)}) custom-call(f32[1,256,128]{2,1,0:T(8,128)} %gen_noise.1, f32[1,256,128]{2,1,0:T(8,128)} %renoise.1, s32[1]{0:T(128)S(6)} %copy.11.gen_step, s32[1]{0:T(128)S(6)} %copy.12.renoise_step, bf16[1,768]{1,0:T(2,128)(2,1)} %text.1, bf16[3,64,3072]{2,1,0:T(8,128)(2,1)} %embed.1, ...), custom_call_target="tpu_custom_call" | custom-call | tf_op jit(solution)/shard_map/distill/pallas_call | solution.py:489
  39.4 2.0 %finish.1 = (f32[192,768]{1,0:T(8,128)}, f32[1,256,128]{2,1,0:T(8,128)}) custom-call(bf16[192,128]{1,0:T(8,128)(2,1)} %get-tuple-element.4.term, bf16[3,64,768]{2,1,0:T(8,128)(2,1)} %unembed.3, f32[1,256,128]{2,1,0:T(8,128)} %get-tuple-element.5.score), custom_call_target="tpu_custom_call" | custom-call | tf_op jit(solution)/shard_map/finish/pallas_call | solution.py:539

commit v4 on v3

--- a/solution.py
+++ b/solution.py
@@ -129,9 +129,6 @@
     ld_mod = [load(mod_weight.at[k], modw_v.at[k], 1 + k) for k in range(3)]
     ld_une = load(unembed, une_v, 4)
     ld_proj = load(proj, proj_v, 5)
-    ld_emb = load(embed, emb_v, 6)
-    ld_noise = load(gen_noise.at[0], noise_v, 7)
-    ld_renoise = load(renoise.at[0], renoise_v, 8)
 
     def plane(dy, dx):
         return {"fsdp": lax.rem(y + dy, NY) * NX + lax.rem(x + dx, NX)}
@@ -177,10 +174,13 @@
     vectors = jnp.concatenate([joined, jnp.zeros_like(joined)], axis=0).astype(BF16)
 
     ld_mod[0].wait()
+    ld_emb = load(embed, emb_v, 6)
     out0 = dot(vectors, modw_v[0])
     ld_mod[1].wait()
     out1 = dot(vectors, modw_v[1])
     ld_mod[2].wait()
+    ld_noise = load(gen_noise.at[0], noise_v, 7)
+    ld_renoise = load(renoise.at[0], renoise_v, 8)
     out2 = dot(vectors, modw_v[2])
     guided = out1[2:3] + GUIDANCE * (out1[1:2] - out1[2:3])
     rows = sublanes((8, WIN))
@@ -214,11 +214,11 @@
     ld_une.wait()
     ld_proj.wait()
     for k in range(3):
-        fold_send[k] = pack_pair(dot_nt(proj_v[k], une_v[k]))
+        fold_send[k] = pack_pair(dot_nt(proj_v[k], une_v[k])).astype(BF16)
     ld_emb.wait()
     for k in range(3):
         own = emb_v[k, :, pl.ds(pl.multiple_of(m * QUARTER, 128), QUARTER)]
-        fold_send[3, 32 * k : 32 * k + 32, :] = pack_pair(dot_nt(own, une_v[k]))
+        fold_send[3, 32 * k : 32 * k + 32, :] = pack_pair(dot_nt(own, une_v[k])).astype(BF16)
     fold_copies = []
     for r in range(1, MP):
         target = lax.rem(m + r, MP)
@@ -243,7 +243,9 @@
 
     for copy in fold_copies:
         copy.wait_recv()
-    folded = fold_send[m] + fold_recv[0] + fold_recv[1] + fold_recv[2]
+    folded = fold_send[m].astype(F32)
+    for r in range(MP - 1):
+        folded = folded + fold_recv[r].astype(F32)
 
     def direct_copy(r):
         return remote(direct_v, direct_v, S_DIRECT + r, {"mp": r}, recv_slot=S_DIRECT)
@@ -504,8 +506,8 @@
             vmem((1, TXT), BF16),
             vmem((8, WIN), F32),
             vmem((2, 8, WIN), F32),
-            vmem((4, HALF, 128), F32),
-            vmem((3, HALF, 128), F32),
+            vmem((4, HALF, 128), BF16),
+            vmem((3, HALF, 128), BF16),
             vmem((HALF, 128), F32),
             vmem((48, 128), BF16),
             vmem((3, 48, 128), BF16),

time: 41.5 us -> 41.3 us (level)
  no operation moved by 1% of the time
where the time goes in v4:
time: 41.3 us; the launch traced here: 41.2 us
  Pallas kernels  39.2 us (95%)
  between operations  1.93 us (5%)
    pallas_call x1, Pallas kernels, body(): pl.pallas_call(kernel, out_shape=(jax.ShapeDtypeStruct((ROWS, 128), BF16)...  37.2 us
    pallas_call x1, Pallas kernels, body(): pl.pallas_call(finish, out_shape=(jax.ShapeDtypeStruct((ROWS, QUARTER), F...  2 us

profile of v4, /device:TPU:1, one launch (start us, length us, event | category | flops | bytes accessed | tf_op | source)
XLA Modules:
  0.0 41.2 jit_solution(6276856166891956193)
XLA Ops:
  1.9 37.2 %distill.1 = (bf16[192,128]{1,0:T(8,128)(2,1)}, f32[1,256,128]{2,1,0:T(8,128)}) custom-call(f32[1,256,128]{2,1,0:T(8,128)} %gen_noise.1, f32[1,256,128]{2,1,0:T(8,128)} %renoise.1, s32[1]{0:T(128)S(6)} %copy.11.gen_step, s32[1]{0:T(128)S(6)} %copy.12.renoise_step, bf16[1,768]{1,0:T(2,128)(2,1)} %text.1, bf16[3,64,3072]{2,1,0:T(8,128)(2,1)} %embed.1, ...), custom_call_target="tpu_custom_call" | custom-call | tf_op jit(solution)/shard_map/distill/pallas_call | solution.py:491
  39.2 2.0 %finish.1 = (f32[192,768]{1,0:T(8,128)}, f32[1,256,128]{2,1,0:T(8,128)}) custom-call(bf16[192,128]{1,0:T(8,128)(2,1)} %get-tuple-element.4.term, bf16[3,64,768]{2,1,0:T(8,128)(2,1)} %unembed.3, f32[1,256,128]{2,1,0:T(8,128)} %get-tuple-element.5.score), custom_call_target="tpu_custom_call" | custom-call | tf_op jit(solution)/shard_map/finish/pallas_call | solution.py:541

commit v5 on v4

--- a/solution.py
+++ b/solution.py
@@ -421,6 +421,20 @@
     score_copy = pltpu.make_async_copy(score_v, score_out.at[0], out_sem.at[0])
     score_copy.start()
 
+    for k in range(2):
+        @pl.when(first + k != f)
+        def _():
+            mod_copy(k).wait_send()
+
+    @pl.when(m == MP - 1)
+    def _():
+        for r in range(MP - 1):
+            direct_copy(r).wait_send()
+
+    for copy in fold_copies + x_copies + y_copies + map_copies + gen_copies + sum_copies:
+        copy.wait_send()
+    score_copy.wait()
+
     for copy in col_copies:
         copy.wait_recv()
     table = [col_v[k].astype(F32) for k in range(DP * MP)]
@@ -436,21 +450,8 @@
     term_copy = pltpu.make_async_copy(term_v, term_out, out_sem.at[1])
     term_copy.start()
 
-    for k in range(2):
-        @pl.when(first + k != f)
-        def _():
-            mod_copy(k).wait_send()
-
-    @pl.when(m == MP - 1)
-    def _():
-        for r in range(MP - 1):
-            direct_copy(r).wait_send()
-
-    for copy in (
-        fold_copies + x_copies + y_copies + map_copies + gen_copies + sum_copies + col_copies
-    ):
+    for copy in col_copies:
         copy.wait_send()
-    score_copy.wait()
     term_copy.wait()
 
 

time: 41.3 us -> 41.3 us (level)
  no operation moved by 1% of the time
where the time goes in v5:
time: 41.3 us; the launch traced here: 41.2 us
  Pallas kernels  39.2 us (95%)
  between operations  1.93 us (5%)
    pallas_call x1, Pallas kernels, body(): pl.pallas_call(kernel, out_shape=(jax.ShapeDtypeStruct((ROWS, 128), BF16)...  37.2 us
    pallas_call x1, Pallas kernels, body(): pl.pallas_call(finish, out_shape=(jax.ShapeDtypeStruct((ROWS, QUARTER), F...  2 us

profile of v5, /device:TPU:1, one launch (start us, length us, event | category | flops | bytes accessed | tf_op | source)
XLA Modules:
  0.0 41.2 jit_solution(5576157549889562976)
XLA Ops:
  1.9 37.2 %distill.1 = (bf16[192,128]{1,0:T(8,128)(2,1)}, f32[1,256,128]{2,1,0:T(8,128)}) custom-call(f32[1,256,128]{2,1,0:T(8,128)} %gen_noise.1, f32[1,256,128]{2,1,0:T(8,128)} %renoise.1, s32[1]{0:T(128)S(6)} %copy.11.gen_step, s32[1]{0:T(128)S(6)} %copy.12.renoise_step, bf16[1,768]{1,0:T(2,128)(2,1)} %text.1, bf16[3,64,3072]{2,1,0:T(8,128)(2,1)} %embed.1, ...), custom_call_target="tpu_custom_call" | custom-call | tf_op jit(solution)/shard_map/distill/pallas_call | solution.py:492
  39.2 2.0 %finish.1 = (f32[192,768]{1,0:T(8,128)}, f32[1,256,128]{2,1,0:T(8,128)}) custom-call(bf16[192,128]{1,0:T(8,128)(2,1)} %get-tuple-element.4.term, bf16[3,64,768]{2,1,0:T(8,128)(2,1)} %unembed.3, f32[1,256,128]{2,1,0:T(8,128)} %get-tuple-element.5.score), custom_call_target="tpu_custom_call" | custom-call | tf_op jit(solution)/shard_map/finish/pallas_call | solution.py:542
